TPU v7x, 512 devices: a whole 4x8x8 slice. The times are simulated.
512 devices in a mesh: segment: 32 (over y_lo, z), dp: 8 (over x, core), seq: 2 (over y_hi).
Axes of the slice: x: 4, y: 8 (y_hi: 2, y_lo: 4; y = y_hi * 4 + y_lo), z: 8, core: 2. Of those that a mesh axis runs over, the one named last changes fastest.
Arguments:
- stored_part_activation: bfloat16 [32, 2, 8, 256, 2048], P('segment', None, 'dp', 'seq'), may hold values from -64 to 64
- pending_sensitivity: bfloat16 [32, 8, 256, 2048], P('segment', 'dp', 'seq'), may hold values from -0.119628906 to 0.119628906
- uppermost_result_derivative: bfloat16 [1, 8, 256, 2048], P(None, 'dp', 'seq'), may hold values from -0.119628906 to 0.119628906
- scaling_factors: float32 [32, 4, 2048], P('segment'), may hold values from -0.5 to 5
- attended_tile_table: int32 [32, 2, 8, 2, 2], P('segment', None, 'dp'), may hold values from 0 to 1, as said below
- active_tile_number: int32 [32, 2, 8, 2], P('segment', None, 'dp'), may hold values from 1 to 2
Outputs:
- factor_derivatives: float32 [32, 4, 2048], P('segment')
Inputs may be any that keep to these rules, and one draw needn't show every extreme that they name: `attended_tile_table`: each list names every key block of its sample once; the allowed ones come first.
All inputs are finite; a program needn't handle non-finite values.
Results may differ from a plain program's by a relative error of at most 0.009.
Values may be sent and summed in bfloat16 or wider, within the bound.
A program may use at most 64 MiB of HBM per device.

v0:
```python
import jax
import jax.numpy as jnp
from jax import lax
from jax.sharding import PartitionSpec as P

HEAD_DIM = 128
BLK = 128
epsilon = 1e-06


def partner(block, axis, apart):
    count = lax.axis_size(axis)
    route = []
    for low in range(count):
        high = low | 1 << apart
        if high != low and high < count:
            route += [(low, high), (high, low)]
    return lax.ppermute(block, axis, route)


def from_behind(block, axis, distance):
    devices = range(lax.axis_size(axis))
    route = [(i - distance, i) for i in devices if i - distance in devices]
    return lax.ppermute(block, axis, route)


def normed_of(inputs):
    widened = inputs.astype(jnp.float32).reshape(
        inputs.shape[:-1] + (inputs.shape[-1] // HEAD_DIM, HEAD_DIM)
    )
    inv_rms = lax.rsqrt(jnp.mean(widened * widened, axis=-1, keepdims=True) + epsilon)
    return (widened * inv_rms, inv_rms)


def norm_back(grad_norm, norm_val, inv_rms):
    return inv_rms * (grad_norm - norm_val * jnp.mean(grad_norm * norm_val, axis=-1, keepdims=True))


def allowed_blocks(block_list, live_count):
    block_total = block_list.shape[0]
    live_slots = jnp.arange(block_total)[None, :] < live_count[:, None]
    matches = (block_list[:, :, None] == jnp.arange(block_total)[None, None, :]) & live_slots[
        :, :, None
    ]
    return jnp.any(matches, axis=1)


def token_mask(permitted, query_half, seq_index, dev_blocks):
    local_blocks = jnp.arange(dev_blocks, dtype=jnp.int32)
    query_rows = query_half * dev_blocks + local_blocks
    key_order = jnp.concatenate(
        [seq_index * dev_blocks + local_blocks, (1 - seq_index) * dev_blocks + local_blocks]
    )
    picked = permitted[query_rows[:, None], key_order[None, :]]
    return jnp.repeat(jnp.repeat(picked, BLK, axis=0), BLK, axis=1)


def attend(query_norm, key_norm, gain_heads, allowed, incoming, scaling):
    queries = (query_norm * gain_heads[0]).astype(jnp.bfloat16)
    key_mat = (key_norm * gain_heads[1]).astype(jnp.bfloat16)
    val_mat = (key_norm * gain_heads[2]).astype(jnp.bfloat16)
    scores = (
        jnp.einsum("thd,shd->hts", queries, key_mat, preferred_element_type=jnp.float32) * scaling
    )
    scores = jnp.where(allowed[None], scores, -jnp.inf)
    exped = jnp.exp(scores - jnp.max(scores, axis=-1, keepdims=True))
    probs = exped / jnp.sum(exped, axis=-1, keepdims=True)
    probs_low = probs.astype(jnp.bfloat16)
    output = jnp.einsum("hts,shd->thd", probs_low, val_mat, preferred_element_type=jnp.float32)
    grad_out = (gain_heads[3] * incoming).astype(jnp.bfloat16)
    grad_probs = jnp.einsum("thd,shd->hts", grad_out, val_mat, preferred_element_type=jnp.float32)
    grad_scores = (
        probs * (grad_probs - jnp.sum(probs * grad_probs, axis=-1, keepdims=True))
    ).astype(jnp.bfloat16)
    return (queries, key_mat, probs_low, output, grad_out, grad_scores)


def shards(
    stored_part_activation,
    pending_sensitivity,
    uppermost_result_derivative,
    scaling_factors,
    attended_tile_table,
    active_tile_number,
):
    segments = lax.axis_size("segment")
    segment_index = lax.axis_index("segment")
    seq_index = lax.axis_index("seq")
    window = stored_part_activation.shape[1]
    row_count = stored_part_activation.shape[3]
    channels = stored_part_activation.shape[4]
    head_count = channels // HEAD_DIM
    dev_blocks = row_count // BLK
    scaling = HEAD_DIM ** (-0.5)
    own_window = stored_part_activation[0, :, 0]
    gain_heads = scaling_factors[0].reshape(4, head_count, HEAD_DIM)
    incoming_sensitivity = pending_sensitivity[0, 0].astype(jnp.float32)
    totals = jnp.zeros((4, head_count, HEAD_DIM), jnp.float32)
    for step_index in range(window):
        own_rows = own_window[step_index]
        other_rows = partner(own_rows, "seq", 0)
        permitted = allowed_blocks(
            attended_tile_table[0, step_index, 0], active_tile_number[0, step_index, 0]
        )
        own_norm, own_inv = normed_of(own_rows)
        other_norm, other_inv = normed_of(other_rows)
        key_norm = jnp.concatenate([own_norm, other_norm], axis=0)
        incoming = incoming_sensitivity.reshape(row_count, head_count, HEAD_DIM)
        own_allowed = token_mask(permitted, seq_index, seq_index, dev_blocks)
        queries, key_mat, probs_low, output, grad_out, grad_scores = attend(
            own_norm, key_norm, gain_heads, own_allowed, incoming, scaling
        )
        grad_query = (
            jnp.einsum("hts,shd->thd", grad_scores, key_mat, preferred_element_type=jnp.float32)
            * scaling
        )
        grad_key = (
            jnp.einsum("hts,thd->shd", grad_scores, queries, preferred_element_type=jnp.float32)
            * scaling
        )
        grad_value = jnp.einsum(
            "hts,thd->shd", probs_low, grad_out, preferred_element_type=jnp.float32
        )
        key_part = grad_key * gain_heads[1] + grad_value * gain_heads[2]
        self_part = key_part[:row_count]
        key_terms = jnp.sum(grad_key * key_norm, axis=0)
        value_terms = jnp.sum(grad_value * key_norm, axis=0)
        if step_index < window - 1:
            lent = norm_back(key_part[row_count:], other_norm, other_inv).astype(jnp.bfloat16)
            returned = partner(lent, "seq", 0).astype(jnp.float32)
        grad_terms = jnp.stack(
            [
                jnp.sum(grad_query * own_norm, axis=0),
                key_terms,
                value_terms,
                jnp.sum(output * incoming, axis=0),
            ]
        )
        totals = totals + grad_terms
        if step_index < window - 1:
            grad_input = (
                incoming
                + norm_back(grad_query * gain_heads[0] + self_part, own_norm, own_inv)
                + returned
            )
            received = from_behind(grad_input.reshape(row_count, channels), "segment", -1)
            incoming_sensitivity = jnp.where(
                segment_index == segments - 1,
                uppermost_result_derivative[step_index, 0].astype(jnp.float32),
                received,
            )
    summed = lax.psum(totals.reshape(4, channels), ("dp", "seq"))
    return summed[None]


def solution(mesh):
    placed = (
        P("segment", None, "dp", "seq", None),
        P("segment", "dp", "seq", None),
        P(None, "dp", "seq", None),
        P("segment", None, None),
        P("segment", None, "dp", None, None),
        P("segment", None, "dp", None),
    )
    return jax.shard_map(
        shards, mesh=mesh, in_specs=placed, out_specs=P("segment", None, None), check_vma=False
    )
```

profile of v0, /device:TPU:24, one launch (start us, length us, event | category | flops | bytes accessed | tf_op | source)
XLA Modules:
  0.0 220.2 jit_solution(2187491883206557950)
XLA Ops:
  0.0 2.7 %slice_convert_fusion = (f32[1,1,1,128,2048]{4,3,2,1,0:T(8,128)}, bf16[128,2048]{1,0:T(8,128)(2,1)}, bf16[128,2048]{1,0:T(8,128)(2,1)}, f32[1,1,1,128,2048]{4,3,2,1,0:T(8,128)S(1)}) fusion(bf16[1,2,1,128,2048]{4,3,2,1,0:T(8,128)(2,1)} %param.6), kind=kLoop, calls=%fused_computation.75 | loop fusion | flops 524288 | bytes 4194304 | tf_op jit(solution)/shard_map/convert_element_type | solution.py:28
  2.7 5.0 %collective-permute-start = (bf16[128,2048]{1,0:T(8,128)(2,1)}, bf16[128,2048]{1,0:T(8,128)(2,1)}, u32[]{:S(2)}, u32[]{:S(2)}) collective-permute-start(bf16[128,2048]{1,0:T(8,128)(2,1)} %get-tuple-element.12), channel_id=1, source_target_pairs={{0,1},{1,0},{2,3},{3,2},{4,5},{5,4},{6,7},{7,6},{8,9},{9,8},{10,11... | collective-permute-start | bytes 1572872 | tf_op jit(solution)/shard_map/ppermute | solution.py:18
  7.8 4.7 %collective-permute-start.1 = (bf16[128,2048]{1,0:T(8,128)(2,1)}, bf16[128,2048]{1,0:T(8,128)(2,1)}, u32[]{:S(2)}, u32[]{:S(2)}) collective-permute-start(bf16[128,2048]{1,0:T(8,128)(2,1)} %get-tuple-element.13), channel_id=1, source_target_pairs={{0,1},{1,0},{2,3},{3,2},{4,5},{5,4},{6,7},{7,6},{8,9},{9,8},{10,11... | collective-permute-start | bytes 1572872 | tf_op jit(solution)/shard_map/ppermute | solution.py:18
  14.8 1.5 copy.58
  16.6 2.3 %copy.53 = f32[1,1,128,2048]{2,3,1,0:T(8,128)} copy(bf16[1,1,128,2048]{3,2,1,0:T(8,128)(2,1)} %param.7) | data formatting | bytes 1572864 | tf_op jit(solution)/shard_map/convert_element_type | solution.py:97
  19.5 1.1 broadcast_multiply_fusion.1
  20.6 12.6 %collective-permute-done = bf16[128,2048]{1,0:T(8,128)(2,1)} collective-permute-done((bf16[128,2048]{1,0:T(8,128)(2,1)}, bf16[128,2048]{1,0:T(8,128)(2,1)}, u32[]{:S(2)}, u32[]{:S(2)}) %collective-permute-start) | collective-permute-done | bytes 524320 | tf_op jit(solution)/shard_map/ppermute | solution.py:18
  33.2 1.2 copy.50
  34.5 1.1 broadcast_multiply_fusion.2
  35.6 3.9 %fusion.49 = (f32[16,128]{1,0:T(8,128)S(1)}, f32[16,128,256]{2,1,0:T(8,128)}) fusion(pred[256]{0:T(512)(128)(4,1)S(1)} %broadcast_bitcast_fusion.1, f32[16,128]{1,0:T(8,128)S(1)} %bitcast.124, f32[128,16,128]{0,2,1:T(8,128)} %broadcast_multiply_fusion.2, f32[128,16,128]{0,2,1:T(8,128)S(1)} %broadcast_multiply_fusion.3, f32[16,128]{1,0:T(8,128)S(1)} %bitcast.119), kind=kOutput, calls=%fused_computation.119 | convolution fusion | flops 138412288 | bytes 4219136 | tf_op jit(solution)/shard_map/sub | solution.py:66
  39.5 2.8 %fusion.26 = f32[16,128,256]{2,1,0:T(8,128)S(1)} fusion(f32[128,16,128]{0,2,1:T(8,128)} %bitcast.110, f32[16,128]{1,0:T(8,128)S(1)} %bitcast.141, f32[16,128,256]{2,1,0:T(8,128)} %get-tuple-element.24, f32[16,128]{1,0:T(8,128)S(1)} %get-tuple-element.23), kind=kOutput, calls=%fused_computation.70 | convolution fusion | flops 135790592 | bytes 5259264 | tf_op jit(solution)/shard_map/hts,thd->shd/dot_general | solution.py:121
  42.7 2.2 multiply_reduce_fusion.1
  45.6 1.9 fusion.5
  47.6 1.9 multiply_reduce_fusion.3
  49.5 1.0 multiply_convert_fusion.7
  50.5 6.3 %collective-permute-start.2 = (bf16[128,16,128]{0,2,1:T(8,128)(2,1)}, bf16[128,16,128]{0,2,1:T(8,128)(2,1)}, u32[]{:S(2)}, u32[]{:S(2)}) collective-permute-start(bf16[128,16,128]{0,2,1:T(8,128)(2,1)} %multiply_convert_fusion.7), channel_id=1, source_target_pairs={{0,1},{1,0},{2,3},{3,2},{4,5},{5,4},{6,7},{7,6},{8,9},{9,8},{10,11... | collective-permute-start | bytes 1572872 | tf_op jit(solution)/shard_map/ppermute | solution.py:18
  56.9 1.2 copy.59
  58.2 22.9 %collective-permute-done.2 = bf16[128,16,128]{0,2,1:T(8,128)(2,1)} collective-permute-done((bf16[128,16,128]{0,2,1:T(8,128)(2,1)}, bf16[128,16,128]{0,2,1:T(8,128)(2,1)}, u32[]{:S(2)}, u32[]{:S(2)}) %collective-permute-start.2) | collective-permute-done | bytes 524320 | tf_op jit(solution)/shard_map/ppermute | solution.py:18
  81.1 3.6 %convert_add_fusion = f32[128,16,128]{0,2,1:T(8,128)} fusion(bf16[128,16,128]{0,2,1:T(8,128)(2,1)} %collective-permute-done.2, f32[128,16,128]{0,2,1:T(8,128)} %bitcast.111, f32[128,16]{0,1:T(8,128)S(1)} %broadcast_multiply_fusion.7, f32[128,16]{0,1:T(8,128)S(1)} %add_rsqrt_fusion.3, f32[256,16,128]{0,2,1:T(8,128)} %copy-done.2, ...), kind=kLoop, calls=%fused_computation.45 | loop fusion | flops 2359296 | bytes 5791744 | tf_op jit(solution)/shard_map/add | solution.py:142
  84.7 2.6 %copy.62 = f32[128,2048]{1,0:T(8,128)} copy(f32[128,2048]{0,1:T(8,128)} %bitcast.114) | data formatting | bytes 2097152 | tf_op jit(solution)/shard_map/reshape | solution.py:146
  87.3 11.7 %collective-permute-start.3 = (f32[128,2048]{1,0:T(8,128)}, f32[128,2048]{1,0:T(8,128)}, u32[]{:S(2)}, u32[]{:S(2)}) collective-permute-start(f32[128,2048]{1,0:T(8,128)} %copy.62), channel_id=1, source_target_pairs={{16,0},{32,16},{48,32},{64,48},{80,64},{96,80},{112,96},{128,112},... | collective-permute-start | bytes 3145736 | tf_op jit(solution)/shard_map/ppermute | solution.py:24
  99.0 1.1 broadcast_multiply_fusion
  100.1 4.8 %fusion.50 = (f32[16,128]{1,0:T(8,128)S(1)}, f32[16,128,256]{2,1,0:T(8,128)}) fusion(pred[256]{0:T(512)(128)(4,1)S(1)} %broadcast_bitcast_fusion, f32[16,128]{1,0:T(8,128)S(1)} %bitcast.126, f32[128,16,128]{0,2,1:T(8,128)} %broadcast_multiply_fusion, f32[128,16,128]{0,2,1:T(8,128)} %broadcast_multiply_fusion.1, f32[16,128]{1,0:T(8,128)S(1)} %bitcast.121), kind=kOutput, calls=%fused_computation.120 | convolution fusion | flops 138412288 | bytes 4219136 | tf_op jit(solution)/shard_map/sub | solution.py:66
  104.9 2.6 %fusion.12 = f32[16,128]{1,0:T(8,128)S(1)} fusion(f32[128,16,128]{0,2,1:T(8,128)S(1)} %bitcast.113, f32[16,128]{1,0:T(8,128)S(1)} %bitcast.133, f32[128,16,128]{0,2,1:T(8,128)S(1)} %copy-done.1, f32[128,16,128]{0,2,1:T(8,128)S(1)} %broadcast_multiply_fusion.3, f32[16,128,256]{2,1,0:T(8,128)} %get-tuple-element.24, f32[16,128]{1,0:T(8,128)S(1)} %get-tuple-element.23), kind=kOutput, calls=%fused_computation.37 | convolution fusion | flops 137361408 | bytes 5267456 | tf_op jit(solution)/shard_map/hts,shd->thd/dot_general | solution.py:69
  107.5 14.2 %collective-permute-done.3 = f32[128,2048]{1,0:T(8,128)} collective-permute-done((f32[128,2048]{1,0:T(8,128)}, f32[128,2048]{1,0:T(8,128)}, u32[]{:S(2)}, u32[]{:S(2)}) %collective-permute-start.3) | collective-permute-done | bytes 1048608 | tf_op jit(solution)/shard_map/ppermute | solution.py:24
  121.7 1.3 convert_select_fusion
  123.1 1.3 copy.63
  124.4 3.4 %multiply_reduce_fusion = (f32[16,128]{1,0:T(8,128)S(1)}, f32[16,128,256]{2,1,0:T(8,128)S(1)}) fusion(f32[16,128,256]{2,1,0:T(8,128)S(1)} %copy-done.6, f32[16,128]{1,0:T(8,128)S(1)} %get-tuple-element.28, f32[16,128]{1,0:T(8,128)S(1)} %bitcast.134, f32[128,16,128]{0,2,1:T(8,128)} %broadcast_multiply_fusion, f32[128,16,128]{0,2,1:T(8,128)} %broadcast_multiply_fusion.1, ...), kind=kOutput, calls=%fused_computation.17 | convolution fusion | flops 137885696 | bytes 7372800 | tf_op jit(solution)/shard_map/thd,shd->hts/dot_general | solution.py:71
  127.8 0.8 multiply_convert_fusion
  131.3 1.1 fusion.2
  132.4 1.2 fusion.14
  133.7 86.5 %psum.7 = f32[1,4,2048]{2,1,0:T(4,128)} all-reduce(f32[1,4,2048]{2,1,0:T(4,128)S(1)} %fusion.32), channel_id=1, replica_groups=mesh['segment'=32,'dp'=8,'seq'=2] {'dp','seq'}, use_global_device_ids=true, to_apply=%region_22.23 | all-reduce | flops 8192 | bytes 65536 | tf_op jit(solution)/shard_map/psum | solution.py:152
  (60 shorter events, 7.1 us)
Async XLA Ops:
  0.0 12.8 %copy-start.13 = (s32[1,2,1,2]{3,2,1,0:T(1,128)S(1)}, s32[1,2,1,2]{3,2,1,0:T(1,128)}, u32[]{:S(2)}) copy-start(s32[1,2,1,2]{3,2,1,0:T(1,128)} %param.11) | copy-start | bytes 52
  0.0 12.8 %copy-start.12 = (s32[1,2,1,2,2]{4,3,2,1,0:T(2,128)S(1)}, s32[1,2,1,2,2]{4,3,2,1,0:T(2,128)}, u32[]{:S(2)}) copy-start(s32[1,2,1,2,2]{4,3,2,1,0:T(2,128)} %param.10) | copy-start | bytes 100
  2.7 30.5 %collective-permute-start = (bf16[128,2048]{1,0:T(8,128)(2,1)}, bf16[128,2048]{1,0:T(8,128)(2,1)}, u32[]{:S(2)}, u32[]{:S(2)}) collective-permute-start(bf16[128,2048]{1,0:T(8,128)(2,1)} %get-tuple-element.12), channel_id=1, source_target_pairs={{0,1},{1,0},{2,3},{3,2},{4,5},{5,4},{6,7},{7,6},{8,9},{9,8},{10,11... | collective-permute-start | bytes 1572872 | tf_op jit(solution)/shard_map/ppermute | solution.py:18
  7.8 49.1 %collective-permute-start.1 = (bf16[128,2048]{1,0:T(8,128)(2,1)}, bf16[128,2048]{1,0:T(8,128)(2,1)}, u32[]{:S(2)}, u32[]{:S(2)}) collective-permute-start(bf16[128,2048]{1,0:T(8,128)(2,1)} %get-tuple-element.13), channel_id=1, source_target_pairs={{0,1},{1,0},{2,3},{3,2},{4,5},{5,4},{6,7},{7,6},{8,9},{9,8},{10,11... | collective-permute-start | bytes 1572872 | tf_op jit(solution)/shard_map/ppermute | solution.py:18
  14.0 0.8 copy-start.11
  39.5 2.9 %copy-start = (f32[128,16,128]{0,2,1:T(8,128)S(1)}, f32[128,16,128]{0,2,1:T(8,128)}, u32[]{:S(2)}) copy-start(f32[128,16,128]{0,2,1:T(8,128)} %broadcast_multiply_fusion.2) | copy-start | bytes 3145732
  39.5 2.9 %copy-start.3 = (f32[1,1,128,2048]{2,3,1,0:T(8,128)S(1)}, f32[1,1,128,2048]{2,3,1,0:T(8,128)}, u32[]{:S(2)}) copy-start(f32[1,1,128,2048]{2,3,1,0:T(8,128)} %copy.53) | copy-start | bytes 3145732
  39.5 3.2 %copy-start.5 = (f32[16,128,256]{2,1,0:T(8,128)S(1)}, f32[16,128,256]{2,1,0:T(8,128)}, u32[]{:S(2)}) copy-start(f32[16,128,256]{2,1,0:T(8,128)} %get-tuple-element.24) | copy-start | bytes 6291460
  47.6 1.9 copy-start.2
  50.5 30.6 %collective-permute-start.2 = (bf16[128,16,128]{0,2,1:T(8,128)(2,1)}, bf16[128,16,128]{0,2,1:T(8,128)(2,1)}, u32[]{:S(2)}, u32[]{:S(2)}) collective-permute-start(bf16[128,16,128]{0,2,1:T(8,128)(2,1)} %multiply_convert_fusion.7), channel_id=1, source_target_pairs={{0,1},{1,0},{2,3},{3,2},{4,5},{5,4},{6,7},{7,6},{8,9},{9,8},{10,11... | collective-permute-start | bytes 1572872 | tf_op jit(solution)/shard_map/ppermute | solution.py:18
  87.3 34.4 %collective-permute-start.3 = (f32[128,2048]{1,0:T(8,128)}, f32[128,2048]{1,0:T(8,128)}, u32[]{:S(2)}, u32[]{:S(2)}) collective-permute-start(f32[128,2048]{1,0:T(8,128)} %copy.62), channel_id=1, source_target_pairs={{16,0},{32,16},{48,32},{64,48},{80,64},{96,80},{112,96},{128,112},... | collective-permute-start | bytes 3145736 | tf_op jit(solution)/shard_map/ppermute | solution.py:24
  100.1 4.8 %copy-start.1 = (f32[128,16,128]{0,2,1:T(8,128)S(1)}, f32[128,16,128]{0,2,1:T(8,128)}, u32[]{:S(2)}) copy-start(f32[128,16,128]{0,2,1:T(8,128)} %broadcast_multiply_fusion.2) | copy-start | bytes 3145732
  100.1 4.8 %copy-start.4 = (f32[1,1,128,2048]{2,3,1,0:T(8,128)S(1)}, f32[1,1,128,2048]{2,3,1,0:T(8,128)}, u32[]{:S(2)}) copy-start(f32[1,1,128,2048]{2,3,1,0:T(8,128)} %copy.53) | copy-start | bytes 3145732
  104.9 16.8 %copy-start.10 = (bf16[1,1,128,2048]{3,2,1,0:T(8,128)(2,1)S(1)}, bf16[1,1,128,2048]{3,2,1,0:T(8,128)(2,1)}, u32[]{:S(2)}) copy-start(bf16[1,1,128,2048]{3,2,1,0:T(8,128)(2,1)} %param.8) | copy-start | bytes 1572868
  107.5 16.9 %copy-start.6 = (f32[16,128,256]{2,1,0:T(8,128)S(1)}, f32[16,128,256]{2,1,0:T(8,128)}, u32[]{:S(2)}) copy-start(f32[16,128,256]{2,1,0:T(8,128)} %get-tuple-element.29) | copy-start | bytes 6291460
  127.8 1.2 copy-start.7
  127.8 1.5 copy-start.8
  130.0 1.2 copy-start.9
where the time goes:
time: 221 us; the launch traced here: 220 us
  blocking collectives  86.5 us (39%)
  waiting for transfers between devices  49.7 us (22%)
  starting transfers between devices  27.7 us (13%)
  matrix products  27.2 us (12%)
  other arithmetic  14.5 us (7%)
  local copies, waits for them, and re-layouts  14.3 us (6%)
    psum x1, blocking collectives, shards(): summed = lax.psum(totals.reshape(4, channels), ('dp', 'seq'))  86.5 us
    ppermute x3, waiting for transfers between devices, partner(): return lax.ppermute(block, axis, route)  35.5 us
    ppermute x3, starting transfers between devices, partner(): return lax.ppermute(block, axis, route)  16 us
    ppermute x1, waiting for transfers between devices, from_behind(): return lax.ppermute(block, axis, route)  14.2 us
    ppermute x1, starting transfers between devices, from_behind(): return lax.ppermute(block, axis, route)  11.7 us
    sub x2, matrix products, attend(): exped = jnp.exp(scores - jnp.max(scores, axis=-1, keepdims=True))  8.66 us
    dot_general x2, matrix products, attend(): jnp.einsum('thd,shd->hts', grad_out, val_mat, preferred_element_type=jnp....  5.55 us
  transfers between devices with their start and end apart: 4, of which 3 were waited for; matrix products, arithmetic and copies ran while one was open for 16% of the time, Pallas kernels for 0%

commit v1 on v0

--- a/solution.py
+++ b/solution.py
@@ -149,7 +149,7 @@
                 uppermost_result_derivative[step_index, 0].astype(jnp.float32),
                 received,
             )
-    summed = lax.psum(totals.reshape(4, channels), ("dp", "seq"))
+    summed = lax.psum(lax.psum(totals.reshape(4, channels), "seq"), "dp")
     return summed[None]
 
 

time: 221 us -> 172 us (0.78)
  the two profiles are of different devices: /device:TPU:24 before, /device:TPU:56 now
where the time goes in v1:
time: 172 us; the launch traced here: 171 us
  waiting for transfers between devices  51 us (30%)
  blocking collectives  39.3 us (23%)
  matrix products  27.2 us (16%)
  starting transfers between devices  24.9 us (14%)
  other arithmetic  14.5 us (8%)
  local copies, waits for them, and re-layouts  14.3 us (8%)
    psum x2, blocking collectives, shards(): summed = lax.psum(lax.psum(totals.reshape(4, channels), 'seq'), 'dp')  39.3 us
    ppermute x3, waiting for transfers between devices, partner(): return lax.ppermute(block, axis, route)  37.9 us
    ppermute x3, starting transfers between devices, partner(): return lax.ppermute(block, axis, route)  13.2 us
    ppermute x1, waiting for transfers between devices, from_behind(): return lax.ppermute(block, axis, route)  13.1 us
    ppermute x1, starting transfers between devices, from_behind(): return lax.ppermute(block, axis, route)  11.7 us
    sub x2, matrix products, attend(): exped = jnp.exp(scores - jnp.max(scores, axis=-1, keepdims=True))  8.66 us
    dot_general x2, matrix products, attend(): jnp.einsum('thd,shd->hts', grad_out, val_mat, preferred_element_type=jnp....  5.55 us
    dot_general x2, matrix products, shards(): jnp.einsum('hts,thd->shd', probs_low, grad_out, preferred_element_type=jn...  4 us
  transfers between devices with their start and end apart: 4, of which 3 were waited for; matrix products, arithmetic and copies ran while one was open for 20% of the time, Pallas kernels for 0%

profile of v1, /device:TPU:56, one launch (start us, length us, event | category | flops | bytes accessed | tf_op | source)
XLA Modules:
  0.0 171.4 jit_solution(16362318808093734765)
XLA Ops:
  0.0 2.7 %slice_convert_fusion = (f32[1,1,1,128,2048]{4,3,2,1,0:T(8,128)}, bf16[128,2048]{1,0:T(8,128)(2,1)}, bf16[128,2048]{1,0:T(8,128)(2,1)}, f32[1,1,1,128,2048]{4,3,2,1,0:T(8,128)S(1)}) fusion(bf16[1,2,1,128,2048]{4,3,2,1,0:T(8,128)(2,1)} %param.6), kind=kLoop, calls=%fused_computation.75 | loop fusion | flops 524288 | bytes 4194304 | tf_op jit(solution)/shard_map/convert_element_type | solution.py:28
  2.7 4.7 %collective-permute-start = (bf16[128,2048]{1,0:T(8,128)(2,1)}, bf16[128,2048]{1,0:T(8,128)(2,1)}, u32[]{:S(2)}, u32[]{:S(2)}) collective-permute-start(bf16[128,2048]{1,0:T(8,128)(2,1)} %get-tuple-element.12), channel_id=1, source_target_pairs={{0,1},{1,0},{2,3},{3,2},{4,5},{5,4},{6,7},{7,6},{8,9},{9,8},{10,11... | collective-permute-start | bytes 1572872 | tf_op jit(solution)/shard_map/ppermute | solution.py:18
  7.4 5.0 %collective-permute-start.1 = (bf16[128,2048]{1,0:T(8,128)(2,1)}, bf16[128,2048]{1,0:T(8,128)(2,1)}, u32[]{:S(2)}, u32[]{:S(2)}) collective-permute-start(bf16[128,2048]{1,0:T(8,128)(2,1)} %get-tuple-element.13), channel_id=1, source_target_pairs={{0,1},{1,0},{2,3},{3,2},{4,5},{5,4},{6,7},{7,6},{8,9},{9,8},{10,11... | collective-permute-start | bytes 1572872 | tf_op jit(solution)/shard_map/ppermute | solution.py:18
  14.8 1.5 copy.58
  16.6 2.3 %copy.53 = f32[1,1,128,2048]{2,3,1,0:T(8,128)} copy(bf16[1,1,128,2048]{3,2,1,0:T(8,128)(2,1)} %param.7) | data formatting | bytes 1572864 | tf_op jit(solution)/shard_map/convert_element_type | solution.py:97
  19.5 1.1 broadcast_multiply_fusion.1
  20.6 13.8 %collective-permute-done = bf16[128,2048]{1,0:T(8,128)(2,1)} collective-permute-done((bf16[128,2048]{1,0:T(8,128)(2,1)}, bf16[128,2048]{1,0:T(8,128)(2,1)}, u32[]{:S(2)}, u32[]{:S(2)}) %collective-permute-start) | collective-permute-done | bytes 524320 | tf_op jit(solution)/shard_map/ppermute | solution.py:18
  34.4 1.2 copy.50
  35.8 1.1 broadcast_multiply_fusion.2
  36.9 3.9 %fusion.48 = (f32[16,128]{1,0:T(8,128)S(1)}, f32[16,128,256]{2,1,0:T(8,128)}) fusion(pred[256]{0:T(512)(128)(4,1)S(1)} %broadcast_bitcast_fusion.1, f32[16,128]{1,0:T(8,128)S(1)} %bitcast.124, f32[128,16,128]{0,2,1:T(8,128)} %broadcast_multiply_fusion.2, f32[128,16,128]{0,2,1:T(8,128)S(1)} %broadcast_multiply_fusion.3, f32[16,128]{1,0:T(8,128)S(1)} %bitcast.119), kind=kOutput, calls=%fused_computation.118 | convolution fusion | flops 138412288 | bytes 4219136 | tf_op jit(solution)/shard_map/sub | solution.py:66
  40.8 2.8 %fusion.26 = f32[16,128,256]{2,1,0:T(8,128)S(1)} fusion(f32[128,16,128]{0,2,1:T(8,128)} %bitcast.109, f32[16,128]{1,0:T(8,128)S(1)} %bitcast.141, f32[16,128,256]{2,1,0:T(8,128)} %get-tuple-element.24, f32[16,128]{1,0:T(8,128)S(1)} %get-tuple-element.23), kind=kOutput, calls=%fused_computation.70 | convolution fusion | flops 135790592 | bytes 5259264 | tf_op jit(solution)/shard_map/hts,thd->shd/dot_general | solution.py:121
  43.9 2.2 %multiply_reduce_fusion.1 = (f32[16,128]{1,0:T(8,128)S(1)}, f32[16,128,256]{2,1,0:T(8,128)S(1)}) fusion(f32[16,128,256]{2,1,0:T(8,128)S(1)} %copy-done.5, f32[16,128]{1,0:T(8,128)S(1)} %get-tuple-element.23, f32[16,128]{1,0:T(8,128)S(1)} %bitcast.131, f32[128,16,128]{0,2,1:T(8,128)S(1)} %copy-done, f32[128,16,128]{0,2,1:T(8,128)S(1)} %broadcast_multiply_fusion.3, ...), kind=kOutput, calls=%fused_computation.23 | convolution fusion | flops 137885696 | bytes 7372800 | tf_op jit(solution)/shard_map/thd,shd->hts/dot_general | solution.py:71
  46.9 1.9 %fusion.5 = (f32[16,128]{1,0:T(8,128)S(1)}, f32[16,128]{1,0:T(8,128)S(1)}, f32[256,16,128]{0,2,1:T(8,128)S(1)}) fusion(f32[128,16,128]{0,2,1:T(8,128)S(1)} %copy-done, f32[128,16,128]{0,2,1:T(8,128)S(1)} %broadcast_multiply_fusion.3, f32[16,128,256]{2,1,0:T(8,128)S(1)} %fusion.26, f32[16,128]{1,0:T(8,128)S(1)} %bitcast.132, ...), kind=kOutput, calls=%fused_computation.15 | convolution fusion | flops 139456512 | bytes 7380992 | tf_op jit(solution)/shard_map/hts,thd->shd/dot_general | solution.py:118
  48.8 1.9 %multiply_reduce_fusion.3 = (f32[128,16]{0,1:T(8,128)S(1)}, f32[128,16]{0,1:T(8,128)S(1)}, f32[16,128]{1,0:T(8,128)S(1)}, f32[16,128,128]{2,1,0:T(8,128)}) fusion(f32[128,16,128]{0,2,1:T(8,128)S(1)} %broadcast_multiply_fusion.3, f32[256,16,128]{0,2,1:T(8,128)S(1)} %get-tuple-element.10, f32[16,128]{1,0:T(8,128)S(1)} %broadcast_multiply_fusion.5, ...), kind=kOutput, calls=%fused_computation.48 | convolution fusion | flops 138143744 | bytes 8429568 | tf_op jit(solution)/shard_map/hts,shd->thd/dot_general | solution.py:114
  50.8 1.0 multiply_convert_fusion.7
  51.8 3.5 %collective-permute-start.2 = (bf16[128,16,128]{0,2,1:T(8,128)(2,1)}, bf16[128,16,128]{0,2,1:T(8,128)(2,1)}, u32[]{:S(2)}, u32[]{:S(2)}) collective-permute-start(bf16[128,16,128]{0,2,1:T(8,128)(2,1)} %multiply_convert_fusion.7), channel_id=1, source_target_pairs={{0,1},{1,0},{2,3},{3,2},{4,5},{5,4},{6,7},{7,6},{8,9},{9,8},{10,11... | collective-permute-start | bytes 1572872 | tf_op jit(solution)/shard_map/ppermute | solution.py:18
  55.3 1.2 copy.59
  56.7 24.1 %collective-permute-done.2 = bf16[128,16,128]{0,2,1:T(8,128)(2,1)} collective-permute-done((bf16[128,16,128]{0,2,1:T(8,128)(2,1)}, bf16[128,16,128]{0,2,1:T(8,128)(2,1)}, u32[]{:S(2)}, u32[]{:S(2)}) %collective-permute-start.2) | collective-permute-done | bytes 524320 | tf_op jit(solution)/shard_map/ppermute | solution.py:18
  80.7 3.6 %convert_add_fusion = f32[128,16,128]{0,2,1:T(8,128)} fusion(bf16[128,16,128]{0,2,1:T(8,128)(2,1)} %collective-permute-done.2, f32[128,16,128]{0,2,1:T(8,128)} %bitcast.110, f32[128,16]{0,1:T(8,128)S(1)} %broadcast_multiply_fusion.7, f32[128,16]{0,1:T(8,128)S(1)} %add_rsqrt_fusion.3, f32[256,16,128]{0,2,1:T(8,128)} %copy-done.2, ...), kind=kLoop, calls=%fused_computation.45 | loop fusion | flops 2359296 | bytes 5791744 | tf_op jit(solution)/shard_map/add | solution.py:142
  84.3 2.6 %copy.62 = f32[128,2048]{1,0:T(8,128)} copy(f32[128,2048]{0,1:T(8,128)} %bitcast.113) | data formatting | bytes 2097152 | tf_op jit(solution)/shard_map/reshape | solution.py:146
  86.9 11.7 %collective-permute-start.3 = (f32[128,2048]{1,0:T(8,128)}, f32[128,2048]{1,0:T(8,128)}, u32[]{:S(2)}, u32[]{:S(2)}) collective-permute-start(f32[128,2048]{1,0:T(8,128)} %copy.62), channel_id=1, source_target_pairs={{16,0},{32,16},{48,32},{64,48},{80,64},{96,80},{112,96},{128,112},... | collective-permute-start | bytes 3145736 | tf_op jit(solution)/shard_map/ppermute | solution.py:24
  98.6 1.1 broadcast_multiply_fusion
  99.7 4.8 %fusion.49 = (f32[16,128]{1,0:T(8,128)S(1)}, f32[16,128,256]{2,1,0:T(8,128)}) fusion(pred[256]{0:T(512)(128)(4,1)S(1)} %broadcast_bitcast_fusion, f32[16,128]{1,0:T(8,128)S(1)} %bitcast.126, f32[128,16,128]{0,2,1:T(8,128)} %broadcast_multiply_fusion, f32[128,16,128]{0,2,1:T(8,128)} %broadcast_multiply_fusion.1, f32[16,128]{1,0:T(8,128)S(1)} %bitcast.121), kind=kOutput, calls=%fused_computation.119 | convolution fusion | flops 138412288 | bytes 4219136 | tf_op jit(solution)/shard_map/sub | solution.py:66
  104.5 2.6 %fusion.12 = f32[16,128]{1,0:T(8,128)S(1)} fusion(f32[128,16,128]{0,2,1:T(8,128)S(1)} %bitcast.112, f32[16,128]{1,0:T(8,128)S(1)} %bitcast.133, f32[128,16,128]{0,2,1:T(8,128)S(1)} %copy-done.1, f32[128,16,128]{0,2,1:T(8,128)S(1)} %broadcast_multiply_fusion.3, f32[16,128,256]{2,1,0:T(8,128)} %get-tuple-element.24, f32[16,128]{1,0:T(8,128)S(1)} %get-tuple-element.23), kind=kOutput, calls=%fused_computation.37 | convolution fusion | flops 137361408 | bytes 5267456 | tf_op jit(solution)/shard_map/hts,shd->thd/dot_general | solution.py:69
  107.1 13.1 %collective-permute-done.3 = f32[128,2048]{1,0:T(8,128)} collective-permute-done((f32[128,2048]{1,0:T(8,128)}, f32[128,2048]{1,0:T(8,128)}, u32[]{:S(2)}, u32[]{:S(2)}) %collective-permute-start.3) | collective-permute-done | bytes 1048608 | tf_op jit(solution)/shard_map/ppermute | solution.py:24
  120.2 1.3 convert_select_fusion
  121.5 1.3 copy.63
  122.9 3.4 %multiply_reduce_fusion = (f32[16,128]{1,0:T(8,128)S(1)}, f32[16,128,256]{2,1,0:T(8,128)S(1)}) fusion(f32[16,128,256]{2,1,0:T(8,128)S(1)} %copy-done.6, f32[16,128]{1,0:T(8,128)S(1)} %get-tuple-element.28, f32[16,128]{1,0:T(8,128)S(1)} %bitcast.134, f32[128,16,128]{0,2,1:T(8,128)} %broadcast_multiply_fusion, f32[128,16,128]{0,2,1:T(8,128)} %broadcast_multiply_fusion.1, ...), kind=kOutput, calls=%fused_computation.17 | convolution fusion | flops 137885696 | bytes 7372800 | tf_op jit(solution)/shard_map/thd,shd->hts/dot_general | solution.py:71
  129.7 1.1 fusion.2
  130.8 1.2 fusion.14
  132.1 15.1 %psum.14 = f32[4,2048]{1,0:T(4,128)S(1)} all-reduce(f32[4,2048]{1,0:T(4,128)S(1)} %maximum_add_fusion), channel_id=1, replica_groups=mesh['segment'=32,'dp'=8,'seq'=2] {'seq'}, use_global_device_ids=true, to_apply=%region_22.23 | all-reduce | flops 8192 | bytes 65536 | tf_op jit(solution)/shard_map/psum | solution.py:152
  147.2 24.2 %psum.15 = f32[1,4,2048]{2,1,0:T(4,128)} all-reduce(f32[1,4,2048]{2,1,0:T(4,128)S(1)} %bitcast.117), channel_id=1, replica_groups=mesh['segment'=32,'dp'=8,'seq'=2] {'dp'}, use_global_device_ids=true, to_apply=%region_23.24 | all-reduce | flops 8192 | bytes 65536 | tf_op jit(solution)/shard_map/psum | solution.py:152
  (61 shorter events, 7.9 us)
Async XLA Ops:
  0.0 12.8 %copy-start.13 = (s32[1,2,1,2]{3,2,1,0:T(1,128)S(1)}, s32[1,2,1,2]{3,2,1,0:T(1,128)}, u32[]{:S(2)}) copy-start(s32[1,2,1,2]{3,2,1,0:T(1,128)} %param.11) | copy-start | bytes 52
  0.0 12.8 %copy-start.12 = (s32[1,2,1,2,2]{4,3,2,1,0:T(2,128)S(1)}, s32[1,2,1,2,2]{4,3,2,1,0:T(2,128)}, u32[]{:S(2)}) copy-start(s32[1,2,1,2,2]{4,3,2,1,0:T(2,128)} %param.10) | copy-start | bytes 100
  2.7 31.7 %collective-permute-start = (bf16[128,2048]{1,0:T(8,128)(2,1)}, bf16[128,2048]{1,0:T(8,128)(2,1)}, u32[]{:S(2)}, u32[]{:S(2)}) collective-permute-start(bf16[128,2048]{1,0:T(8,128)(2,1)} %get-tuple-element.12), channel_id=1, source_target_pairs={{0,1},{1,0},{2,3},{3,2},{4,5},{5,4},{6,7},{7,6},{8,9},{9,8},{10,11... | collective-permute-start | bytes 1572872 | tf_op jit(solution)/shard_map/ppermute | solution.py:18
  7.4 47.9 %collective-permute-start.1 = (bf16[128,2048]{1,0:T(8,128)(2,1)}, bf16[128,2048]{1,0:T(8,128)(2,1)}, u32[]{:S(2)}, u32[]{:S(2)}) collective-permute-start(bf16[128,2048]{1,0:T(8,128)(2,1)} %get-tuple-element.13), channel_id=1, source_target_pairs={{0,1},{1,0},{2,3},{3,2},{4,5},{5,4},{6,7},{7,6},{8,9},{9,8},{10,11... | collective-permute-start | bytes 1572872 | tf_op jit(solution)/shard_map/ppermute | solution.py:18
  14.0 0.8 copy-start.11
  40.8 2.9 %copy-start = (f32[128,16,128]{0,2,1:T(8,128)S(1)}, f32[128,16,128]{0,2,1:T(8,128)}, u32[]{:S(2)}) copy-start(f32[128,16,128]{0,2,1:T(8,128)} %broadcast_multiply_fusion.2) | copy-start | bytes 3145732
  40.8 2.9 %copy-start.3 = (f32[1,1,128,2048]{2,3,1,0:T(8,128)S(1)}, f32[1,1,128,2048]{2,3,1,0:T(8,128)}, u32[]{:S(2)}) copy-start(f32[1,1,128,2048]{2,3,1,0:T(8,128)} %copy.53) | copy-start | bytes 3145732
  40.8 3.2 %copy-start.5 = (f32[16,128,256]{2,1,0:T(8,128)S(1)}, f32[16,128,256]{2,1,0:T(8,128)}, u32[]{:S(2)}) copy-start(f32[16,128,256]{2,1,0:T(8,128)} %get-tuple-element.24) | copy-start | bytes 6291460
  48.8 1.9 %copy-start.2 = (f32[256,16,128]{0,2,1:T(8,128)}, f32[256,16,128]{0,2,1:T(8,128)S(1)}, u32[]{:S(2)}) copy-start(f32[256,16,128]{0,2,1:T(8,128)S(1)} %get-tuple-element.10) | copy-start | bytes 6291460
  51.8 29.0 %collective-permute-start.2 = (bf16[128,16,128]{0,2,1:T(8,128)(2,1)}, bf16[128,16,128]{0,2,1:T(8,128)(2,1)}, u32[]{:S(2)}, u32[]{:S(2)}) collective-permute-start(bf16[128,16,128]{0,2,1:T(8,128)(2,1)} %multiply_convert_fusion.7), channel_id=1, source_target_pairs={{0,1},{1,0},{2,3},{3,2},{4,5},{5,4},{6,7},{7,6},{8,9},{9,8},{10,11... | collective-permute-start | bytes 1572872 | tf_op jit(solution)/shard_map/ppermute | solution.py:18
  86.9 33.2 %collective-permute-start.3 = (f32[128,2048]{1,0:T(8,128)}, f32[128,2048]{1,0:T(8,128)}, u32[]{:S(2)}, u32[]{:S(2)}) collective-permute-start(f32[128,2048]{1,0:T(8,128)} %copy.62), channel_id=1, source_target_pairs={{16,0},{32,16},{48,32},{64,48},{80,64},{96,80},{112,96},{128,112},... | collective-permute-start | bytes 3145736 | tf_op jit(solution)/shard_map/ppermute | solution.py:24
  99.7 4.8 %copy-start.1 = (f32[128,16,128]{0,2,1:T(8,128)S(1)}, f32[128,16,128]{0,2,1:T(8,128)}, u32[]{:S(2)}) copy-start(f32[128,16,128]{0,2,1:T(8,128)} %broadcast_multiply_fusion.2) | copy-start | bytes 3145732
  99.7 4.8 %copy-start.4 = (f32[1,1,128,2048]{2,3,1,0:T(8,128)S(1)}, f32[1,1,128,2048]{2,3,1,0:T(8,128)}, u32[]{:S(2)}) copy-start(f32[1,1,128,2048]{2,3,1,0:T(8,128)} %copy.53) | copy-start | bytes 3145732
  104.5 15.7 %copy-start.10 = (bf16[1,1,128,2048]{3,2,1,0:T(8,128)(2,1)S(1)}, bf16[1,1,128,2048]{3,2,1,0:T(8,128)(2,1)}, u32[]{:S(2)}) copy-start(bf16[1,1,128,2048]{3,2,1,0:T(8,128)(2,1)} %param.8) | copy-start | bytes 1572868
  107.1 15.8 %copy-start.6 = (f32[16,128,256]{2,1,0:T(8,128)S(1)}, f32[16,128,256]{2,1,0:T(8,128)}, u32[]{:S(2)}) copy-start(f32[16,128,256]{2,1,0:T(8,128)} %get-tuple-element.29) | copy-start | bytes 6291460
  126.2 1.2 copy-start.7
  126.2 1.5 copy-start.8
  128.5 1.2 copy-start.9
